TPU v7x, 32 devices: a whole 2x2x4 slice. The times are simulated.
32 devices in a mesh: dp: 16 (over z, y, core), tensor: 2 (over x).
Axes of the slice: x: 2, y: 2, z: 4, core: 2. Of those that a mesh axis runs over, the one named last changes fastest.
Arguments:
- hidden_in: bfloat16 [2, 8192, 1024], P(None, ('dp', 'tensor')), may hold values from -6 to 6
- segment_ids: int32 [2, 16, 512], P(None, 'dp'), may hold values from 0 to 3, never falling along the last dimension, each value on 1 to 256 neighbouring positions
- out_grad: bfloat16 [2, 8192, 1024], P(None, ('dp', 'tensor')), may hold values from -6 to 6
- w_query: bfloat16 [1024, 1024], P(None, 'tensor'), may hold values from -0.1875 to 0.1875
- b_query: bfloat16 [1024], P('tensor'), may hold values from -1.75 to 1.75
- w_key: bfloat16 [1024, 1024], P(None, 'tensor'), may hold values from -0.1875 to 0.1875
- w_value: bfloat16 [1024, 1024], P(None, 'tensor'), may hold values from -0.1875 to 0.1875
- b_value: bfloat16 [1024], P('tensor'), may hold values from -1.75 to 1.75
- w_out: bfloat16 [1024, 1024], P('tensor'), may hold values from -0.75 to 0.75
- b_out: bfloat16 [1024], replicated, may hold values from -1.75 to 1.75
- attn_gain: bfloat16 [1024], replicated, may hold values from 0.099609375 to 1.8984375
- attn_shift: bfloat16 [1024], replicated, may hold values from -3 to 3
- w_up: bfloat16 [1024, 4096], P(None, 'tensor'), may hold values from -0.1875 to 0.1875
- b_up: bfloat16 [4096], P('tensor'), may hold values from -1.75 to 1.75
- w_down: bfloat16 [4096, 1024], P('tensor'), may hold values from -0.09375 to 0.09375
- b_down: bfloat16 [1024], replicated, may hold values from -1.75 to 1.75
- ffn_gain: bfloat16 [1024], replicated, may hold values from 0.099609375 to 1.8984375
- ffn_shift: bfloat16 [1024], replicated, may hold values from -3 to 3
Outputs:
- output: bfloat16 [2, 8192, 1024], P(None, ('dp', 'tensor'))
- grad_input: bfloat16 [2, 8192, 1024], P(None, ('dp', 'tensor'))
- grad_w_query: float32 [1024, 1024], P('dp', 'tensor')
- grad_b_query: float32 [1024], P('tensor')
- grad_w_key: float32 [1024, 1024], P('dp', 'tensor')
- grad_w_value: float32 [1024, 1024], P('dp', 'tensor')
- grad_b_value: float32 [1024], P('tensor')
- grad_w_out: float32 [1024, 1024], P('tensor', 'dp')
- grad_b_out: float32 [1024], replicated
- grad_attn_gain: float32 [1024], replicated
- grad_attn_shift: float32 [1024], replicated
- grad_w_up: float32 [1024, 4096], P('dp', 'tensor')
- grad_b_up: float32 [4096], P('tensor')
- grad_w_down: float32 [4096, 1024], P('tensor', 'dp')
- grad_b_down: float32 [1024], replicated
- grad_ffn_gain: float32 [1024], replicated
- grad_ffn_shift: float32 [1024], replicated
Inputs may be any that keep to these rules, and one draw needn't show every extreme that they name: `segment_ids`: along each packed row the ids never fall, every id from 0 to 3 occurs, and each covers 1 to 256 tokens; a token attends only to tokens of its own row with its own id.
All inputs are finite; a program needn't handle non-finite values.
Results may differ from a plain program's by a relative error of at most 0.02.
Values may be sent and summed in bfloat16 or wider, within the bound.
No kernel may reach another device: no remote copies, remote signals or barrier semaphores. Data moves between devices by JAX's collectives and lax.ppermute only.
A program may use at most 192 MiB of HBM per device.

v0:
```python
from functools import reduce
import math
import jax
import jax.numpy as jnp
from jax import lax
from jax.sharding import PartitionSpec as P

HD = 64
MICRO = 2


def layer_norm(inputs, scale_vec, offset):
    centre = inputs - jnp.mean(inputs, axis=-1, keepdims=True)
    spread = jnp.mean(centre * centre, axis=-1, keepdims=True)
    return centre * lax.rsqrt(spread + 1e-12) * scale_vec + offset


def gelu_exact(inputs):
    return jax.nn.gelu(inputs, approximate=False)


def matmul(former, latter):
    return jnp.dot(former, latter, preferred_element_type=jnp.float32)


def inner_rows(former, latter):
    return lax.dot_general(
        former, latter, (((0,), (0,)), ((), ())), preferred_element_type=jnp.float32
    )


def inner_cols(former, latter):
    return lax.dot_general(
        former, latter, (((1,), (1,)), ((), ())), preferred_element_type=jnp.float32
    )


def head_split(block):
    return block.reshape(block.shape[0], block.shape[1] // HD, HD)


def masked_scores(queries, key_rows, seg_row):
    scores = jnp.einsum(
        "qhd,khd->hqk",
        head_split(queries),
        head_split(key_rows),
        preferred_element_type=jnp.float32,
    ) * (1.0 / math.sqrt(HD))
    same_doc = seg_row[:, None] == seg_row[None, :]
    return jnp.where(same_doc[None], scores, -1e30)


def attend_row(packed):
    queries, key_rows, value_rows, seg_row = packed
    scores = masked_scores(queries, key_rows, seg_row)
    highest = jnp.max(scores, axis=-1, keepdims=True)
    logsum = highest + jnp.log(jnp.sum(jnp.exp(scores - highest), axis=-1, keepdims=True))
    probs_low = jnp.exp(scores - logsum).astype(jnp.bfloat16)
    context = jnp.einsum(
        "hqk,khd->qhd", probs_low, head_split(value_rows), preferred_element_type=jnp.float32
    )
    return (context.reshape(queries.shape).astype(jnp.bfloat16), logsum[..., 0])


def attend_back(packed):
    queries, key_rows, value_rows, seg_row, logsum, grad_ctx = packed
    scores = masked_scores(queries, key_rows, seg_row)
    probs = jnp.exp(scores - logsum[..., None])
    grad_heads = head_split(grad_ctx)
    grad_probs = jnp.einsum(
        "qhd,khd->hqk", grad_heads, head_split(value_rows), preferred_element_type=jnp.float32
    )
    centred = grad_probs - jnp.sum(probs * grad_probs, axis=-1, keepdims=True)
    grad_scores = (probs * centred * (1.0 / math.sqrt(HD))).astype(jnp.bfloat16)
    grad_query = jnp.einsum(
        "hqk,khd->qhd", grad_scores, head_split(key_rows), preferred_element_type=jnp.float32
    )
    grad_key = jnp.einsum(
        "hqk,qhd->khd", grad_scores, head_split(queries), preferred_element_type=jnp.float32
    )
    grad_value = jnp.einsum(
        "hqk,qhd->khd", probs.astype(jnp.bfloat16), grad_heads, preferred_element_type=jnp.float32
    )
    flat_shape = queries.shape
    return jnp.concatenate(
        [
            grad_query.reshape(flat_shape),
            grad_key.reshape(flat_shape),
            grad_value.reshape(flat_shape),
        ],
        axis=1,
    ).astype(jnp.bfloat16)


def add_trees(former, latter):
    return jax.tree.map(jnp.add, former, latter)


def on_device(
    hidden_in,
    segment_ids,
    out_grad,
    w_query,
    b_query,
    w_key,
    w_value,
    b_value,
    w_out,
    b_out,
    attn_gain,
    attn_shift,
    w_up,
    b_up,
    w_down,
    b_down,
    ffn_gain,
    ffn_shift,
):
    local_width = w_query.shape[1]
    packed_rows = segment_ids.shape[1]
    length = segment_ids.shape[2]
    w_qkv = jnp.concatenate([w_query, w_key, w_value], axis=1)
    b_qkv = jnp.concatenate([b_query, jnp.zeros_like(b_query), b_value]).astype(jnp.float32)
    b_out32 = b_out.astype(jnp.float32)
    b_up32 = b_up.astype(jnp.float32)
    b_down32 = b_down.astype(jnp.float32)
    attn_gain32 = attn_gain.astype(jnp.float32)
    attn_shift32 = attn_shift.astype(jnp.float32)
    ffn_gain32 = ffn_gain.astype(jnp.float32)
    ffn_shift32 = ffn_shift.astype(jnp.float32)

    def to_rows(block):
        return block.reshape(packed_rows, length, block.shape[1])

    outputs = []
    input_grads = []
    weight_terms = []
    small_terms = []
    for micro_step in range(MICRO):
        tokens_low = hidden_in[micro_step]
        tokens = tokens_low.astype(jnp.float32)
        seg_rows = segment_ids[micro_step]
        full_rows = lax.all_gather(tokens_low, "tensor", axis=0, tiled=True)
        qkv_low = (matmul(full_rows, w_qkv) + b_qkv).astype(jnp.bfloat16)
        queries = qkv_low[:, :local_width]
        key_rows = qkv_low[:, local_width : 2 * local_width]
        value_rows = qkv_low[:, 2 * local_width :]
        context, logsums = lax.map(
            attend_row, (to_rows(queries), to_rows(key_rows), to_rows(value_rows), seg_rows)
        )
        context = context.reshape(-1, local_width)
        attn_part = lax.psum_scatter(
            matmul(context, w_out).astype(jnp.bfloat16), "tensor", scatter_dimension=0, tiled=True
        ).astype(jnp.float32)
        resid_one = attn_part + b_out32 + tokens
        hidden_one, norm_one_back = jax.vjp(layer_norm, resid_one, attn_gain32, attn_shift32)
        hidden_low = hidden_one.astype(jnp.bfloat16)
        hidden_rows = lax.all_gather(hidden_low, "tensor", axis=0, tiled=True)
        pre_act = matmul(hidden_rows, w_up) + b_up32
        activation, gelu_back = jax.vjp(gelu_exact, pre_act)
        gelu_low = activation.astype(jnp.bfloat16)
        ffn_part = lax.psum_scatter(
            matmul(gelu_low, w_down).astype(jnp.bfloat16), "tensor", scatter_dimension=0, tiled=True
        ).astype(jnp.float32)
        resid_two = ffn_part + b_down32 + hidden_one
        result, norm_two_back = jax.vjp(layer_norm, resid_two, ffn_gain32, ffn_shift32)
        outputs.append(result.astype(jnp.bfloat16))
        grad_two, grad_ffn_gain, grad_ffn_shift = norm_two_back(
            out_grad[micro_step].astype(jnp.float32)
        )
        grad_two_low = grad_two.astype(jnp.bfloat16)
        grad_two_rows = lax.all_gather(grad_two_low, "tensor", axis=0, tiled=True)
        grad_down = inner_rows(gelu_low, grad_two_rows)
        grad_act = inner_cols(grad_two_rows, w_down)
        grad_pre = gelu_back(grad_act)[0].astype(jnp.bfloat16)
        grad_up = inner_rows(hidden_rows, grad_pre)
        grad_hidden = (
            lax.psum_scatter(
                inner_cols(grad_pre, w_up).astype(jnp.bfloat16),
                "tensor",
                scatter_dimension=0,
                tiled=True,
            ).astype(jnp.float32)
            + grad_two
        )
        grad_one, grad_attn_gain, grad_attn_shift = norm_one_back(grad_hidden)
        grad_one_low = grad_one.astype(jnp.bfloat16)
        grad_one_rows = lax.all_gather(grad_one_low, "tensor", axis=0, tiled=True)
        grad_wout = inner_rows(context, grad_one_rows)
        grad_ctx = inner_cols(grad_one_rows, w_out).astype(jnp.bfloat16)
        grad_qkv = lax.map(
            attend_back,
            (
                to_rows(queries),
                to_rows(key_rows),
                to_rows(value_rows),
                seg_rows,
                logsums,
                to_rows(grad_ctx),
            ),
        )
        grad_qkv = grad_qkv.reshape(-1, 3 * local_width)
        grad_wqkv = inner_rows(full_rows, grad_qkv)
        grad_in = (
            lax.psum_scatter(
                inner_cols(grad_qkv, w_qkv).astype(jnp.bfloat16),
                "tensor",
                scatter_dimension=0,
                tiled=True,
            ).astype(jnp.float32)
            + grad_one
        )
        input_grads.append(grad_in.astype(jnp.bfloat16))
        small_terms.append(
            (
                jnp.sum(grad_qkv.astype(jnp.float32), axis=0),
                jnp.sum(grad_pre.astype(jnp.float32), axis=0),
                jnp.sum(grad_one, axis=0),
                grad_attn_gain,
                grad_attn_shift,
                jnp.sum(grad_two, axis=0),
                grad_ffn_gain,
                grad_ffn_shift,
            )
        )
        weight_set = (grad_wqkv, grad_up, grad_wout, grad_down)
        weight_terms.append(weight_set)
    summed = reduce(add_trees, weight_terms)
    summed = (
        lax.psum_scatter(
            summed[0].astype(jnp.bfloat16), "dp", scatter_dimension=0, tiled=True
        ).astype(jnp.float32),
        lax.psum_scatter(
            summed[1].astype(jnp.bfloat16), "dp", scatter_dimension=0, tiled=True
        ).astype(jnp.float32),
        lax.psum_scatter(
            summed[2].astype(jnp.bfloat16), "dp", scatter_dimension=1, tiled=True
        ).astype(jnp.float32),
        lax.psum_scatter(
            summed[3].astype(jnp.bfloat16), "dp", scatter_dimension=1, tiled=True
        ).astype(jnp.float32),
    )
    red_qkv, red_up, red_wout, red_down = summed
    small = reduce(add_trees, small_terms)
    bias_qkv, bias_up = lax.psum((small[0], small[1]), "dp")
    norm_bout, norm_again, norm_ashift, norm_bdown, norm_fgain, norm_fshift = lax.psum(
        (small[2], small[3], small[4], small[5], small[6], small[7]), ("dp", "tensor")
    )
    output = jnp.stack(outputs, axis=0)
    grad_input = jnp.stack(input_grads, axis=0)
    return (
        output,
        grad_input,
        red_qkv[:, :local_width],
        bias_qkv[:local_width],
        red_qkv[:, local_width : 2 * local_width],
        red_qkv[:, 2 * local_width :],
        bias_qkv[2 * local_width :],
        red_wout,
        norm_bout,
        norm_again,
        norm_ashift,
        red_up,
        bias_up,
        red_down,
        norm_bdown,
        norm_fgain,
        norm_fshift,
    )


def solution(mesh):
    placed = (
        P(None, ("dp", "tensor"), None),
        P(None, "dp", None),
        P(None, ("dp", "tensor"), None),
        P(None, "tensor"),
        P("tensor"),
        P(None, "tensor"),
        P(None, "tensor"),
        P("tensor"),
        P("tensor", None),
        P(),
        P(),
        P(),
        P(None, "tensor"),
        P("tensor"),
        P("tensor", None),
        P(),
        P(),
        P(),
    )
    return jax.shard_map(
        on_device,
        mesh=mesh,
        in_specs=placed,
        out_specs=(
            P(None, ("dp", "tensor"), None),
            P(None, ("dp", "tensor"), None),
            P("dp", "tensor"),
            P("tensor"),
            P("dp", "tensor"),
            P("dp", "tensor"),
            P("tensor"),
            P("tensor", "dp"),
            P(),
            P(),
            P(),
            P("dp", "tensor"),
            P("tensor"),
            P("tensor", "dp"),
            P(),
            P(),
            P(),
        ),
        check_vma=False,
    )
```

profile of v0, /device:TPU:0, one launch (start us, length us, event | category | flops | bytes accessed | tf_op | source)
XLA Modules:
  0.0 747.1 jit_solution(17031704158051512009)
XLA Ops:
  14.8 19.4 %all-gather.25.cloned.1.call-done = bf16[1,512,1024]{2,1,0:T(8,128)(2,1)} async-done(((bf16[1,256,1024]{2,1,0:T(8,128)(2,1)}), bf16[1,512,1024]{2,1,0:T(8,128)(2,1)}) %all-gather.25.cloned.1.call-update) | async-done | bytes 1048592 | tf_op jit(solution)/shard_map/all_gather | solution.py:143
  34.2 4.1 fusion.71
  38.5 19.2 %all-gather.23.cloned.1.call-done = bf16[1,512,1024]{2,1,0:T(8,128)(2,1)} async-done(((bf16[1,256,1024]{2,1,0:T(8,128)(2,1)}), bf16[1,512,1024]{2,1,0:T(8,128)(2,1)}) %all-gather.23.cloned.1.call-update) | async-done | bytes 1048592 | tf_op jit(solution)/shard_map/all_gather | solution.py:143
  57.7 4.1 fusion.72
  81.6 10.4 %reduce-scatter.15.cloned.1.call-done = bf16[256,1024]{1,0:T(8,128)(2,1)} async-done(((bf16[512,1024]{1,0:T(8,128)(2,1)}), bf16[256,1024]{1,0:T(8,128)(2,1)}) %reduce-scatter.15.cloned.1.call-update) | async-done | bytes 524304 | tf_op jit(solution)/shard_map/reduce_scatter | solution.py:152
  93.5 21.7 %reduce-scatter.19.cloned.1.call-done = bf16[256,1024]{1,0:T(8,128)(2,1)} async-done(((bf16[512,1024]{1,0:T(8,128)(2,1)}), bf16[256,1024]{1,0:T(8,128)(2,1)}) %reduce-scatter.19.cloned.1.call-update) | async-done | bytes 524304 | tf_op jit(solution)/shard_map/reduce_scatter | solution.py:152
  118.3 2.6 fusion.106
  122.0 20.4 %all-gather.13.cloned.1.call-done = bf16[512,1024]{1,0:T(8,128)(2,1)} async-done(((bf16[256,1024]{1,0:T(8,128)(2,1)}), bf16[512,1024]{1,0:T(8,128)(2,1)}) %all-gather.13.cloned.1.call-update) | async-done | bytes 1048592 | tf_op jit(solution)/shard_map/all_gather | solution.py:158
  142.4 6.8 fusion.156
  149.1 16.5 %all-gather.11.cloned.1.call-done = bf16[512,1024]{1,0:T(8,128)(2,1)} async-done(((bf16[256,1024]{1,0:T(8,128)(2,1)}), bf16[512,1024]{1,0:T(8,128)(2,1)}) %all-gather.11.cloned.1.call-update) | async-done | bytes 1048592 | tf_op jit(solution)/shard_map/all_gather | solution.py:158
  165.7 24.0 %multiply_convert_fusion.3 = (bf16[512,2048]{1,0:T(8,128)(2,1)S(1)}, f32[512,2048]{1,0:T(8,128)}, bf16[512,2048]{1,0:T(8,128)(2,1)}, f32[512,2048]{1,0:T(8,128)}, f32[512,2048]{1,0:T(8,128)}) fusion(f32[2048]{0:T(1024)S(1)} %convert_element_type.251, f32[512,2048]{1,0:T(8,128)} %fusion.156, bf16[512,1024]{1,0:T(8,128)(2,1)} %all-gather.11.cloned.1.call-done, ...), kind=kOutput, calls=%fused_computation.48 | convolution fusion | flops 2285895680 | bytes 26222592 | tf_op jit(solution)/shard_map/dot_general | solution.py:23
  191.0 3.3 convolution_convert_fusion.7
  194.4 6.2 convolution_convert_fusion.6
  200.9 13.9 %reduce-scatter.17.cloned.1.call-done = bf16[256,1024]{1,0:T(8,128)(2,1)} async-done(((bf16[512,1024]{1,0:T(8,128)(2,1)}), bf16[256,1024]{1,0:T(8,128)(2,1)}) %reduce-scatter.17.cloned.1.call-update) | async-done | bytes 524304 | tf_op jit(solution)/shard_map/reduce_scatter | solution.py:162
  214.8 23.3 %reduce-scatter.21.cloned.1.call-done = bf16[256,1024]{1,0:T(8,128)(2,1)} async-done(((bf16[512,1024]{1,0:T(8,128)(2,1)}), bf16[256,1024]{1,0:T(8,128)(2,1)}) %reduce-scatter.21.cloned.1.call-update) | async-done | bytes 524304 | tf_op jit(solution)/shard_map/reduce_scatter | solution.py:162
  248.0 19.2 %all-gather.15.cloned.1.call-done = bf16[512,1024]{1,0:T(8,128)(2,1)} async-done(((bf16[256,1024]{1,0:T(8,128)(2,1)}), bf16[512,1024]{1,0:T(8,128)(2,1)}) %all-gather.15.cloned.1.call-update) | async-done | bytes 1048592 | tf_op jit(solution)/shard_map/all_gather | solution.py:172
  267.2 6.9 fusion.157
  274.1 15.8 %all-gather.19.cloned.1.call-done = bf16[512,1024]{1,0:T(8,128)(2,1)} async-done(((bf16[256,1024]{1,0:T(8,128)(2,1)}), bf16[512,1024]{1,0:T(8,128)(2,1)}) %all-gather.19.cloned.1.call-update) | async-done | bytes 1048592 | tf_op jit(solution)/shard_map/all_gather | solution.py:172
  289.9 13.2 %convert_reduce_fusion = (f32[2048]{0:T(1024)S(1)}, bf16[512,2048]{1,0:T(8,128)(2,1)S(1)}, f32[2048]{0:T(1024)S(1)}, bf16[512,2048]{1,0:T(8,128)(2,1)}) fusion(f32[512,2048]{1,0:T(8,128)} %get-tuple-element.221, f32[512,2048]{1,0:T(8,128)} %fusion.156, f32[2048]{0:T(1024)S(1)} %convert_element_type.251, f32[512,2048]{1,0:T(8,128)} %fusion.157, ...), kind=kOutput, calls=%fused_computation.29 | convolution fusion | flops 2183131136 | bytes 30433280 | tf_op jit(solution)/shard_map/dot_general | solution.py:33
  304.5 3.4 convolution_convert_fusion.4
  307.9 6.2 convolution_convert_fusion.5
  314.2 14.1 %reduce-scatter.27.cloned.1.call-done = bf16[256,1024]{1,0:T(8,128)(2,1)} async-done(((bf16[512,1024]{1,0:T(8,128)(2,1)}), bf16[256,1024]{1,0:T(8,128)(2,1)}) %reduce-scatter.27.cloned.1.call-update) | async-done | bytes 524304 | tf_op jit(solution)/shard_map/reduce_scatter | solution.py:178
  328.3 22.5 %reduce-scatter.23.cloned.1.call-done = bf16[256,1024]{1,0:T(8,128)(2,1)} async-done(((bf16[512,1024]{1,0:T(8,128)(2,1)}), bf16[256,1024]{1,0:T(8,128)(2,1)}) %reduce-scatter.23.cloned.1.call-update) | async-done | bytes 524304 | tf_op jit(solution)/shard_map/reduce_scatter | solution.py:178
  350.9 3.3 multiply_reduce_fusion.3
  360.7 19.2 %all-gather.17.cloned.1.call-done = bf16[512,1024]{1,0:T(8,128)(2,1)} async-done(((bf16[256,1024]{1,0:T(8,128)(2,1)}), bf16[512,1024]{1,0:T(8,128)(2,1)}) %all-gather.17.cloned.1.call-update) | async-done | bytes 1048592 | tf_op jit(solution)/shard_map/all_gather | solution.py:188
  382.0 21.2 %all-gather.21.cloned.1.call-done = bf16[512,1024]{1,0:T(8,128)(2,1)} async-done(((bf16[256,1024]{1,0:T(8,128)(2,1)}), bf16[512,1024]{1,0:T(8,128)(2,1)}) %all-gather.21.cloned.1.call-update) | async-done | bytes 1048592 | tf_op jit(solution)/shard_map/all_gather | solution.py:188
  403.1 3.1 add_convert_fusion.5
  409.5 4.5 fusion.158
  414.0 13.8 %fusion.83 = bf16[8,64,512]{2,1,0:T(8,128)(2,1)S(1)} fusion(bf16[512,8,64]{0,2,1:T(8,128)(2,1)S(1)} %bitcast.203, f32[8,512,512]{1,2,0:T(8,128)} %fusion.158, f32[8,512,512]{1,2,0:T(8,128)} %copy-done.3, f32[8,512]{1,0:T(8,128)S(1)} %log_add_fusion.1, pred[512,512]{0,1:T(8,128)(4,1)S(1)} %copy-done.14), kind=kOutput, calls=%fused_computation.115 | convolution fusion | flops 291770880 | bytes 18104320 | tf_op jit(solution)/shard_map/while/body/eval_jaxpr/hqk,khd->qhd/dot_general | solution.py:75
  427.8 14.5 %fusion.86 = bf16[8,64,512]{2,1,0:T(8,128)(2,1)} fusion(bf16[512,8,64]{0,2,1:T(8,128)(2,1)S(1)} %bitcast.201, f32[8,512,512]{1,2,0:T(8,128)} %fusion.158, f32[8,512,512]{1,2,0:T(8,128)} %copy-done.3, f32[8,512]{1,0:T(8,128)S(1)} %log_add_fusion.1, pred[512,512]{0,1:T(8,128)(4,1)S(1)} %copy-done.14), kind=kOutput, calls=%fused_computation.116 | convolution fusion | flops 291770880 | bytes 18104320 | tf_op jit(solution)/shard_map/while/body/eval_jaxpr/hqk,qhd->khd/dot_general | solution.py:78
  442.3 5.7 convolution_convert_fusion.9
  448.9 2.9 convolution_convert_fusion.1
  453.5 4.5 fusion.159
  458.0 13.3 %fusion.77 = bf16[8,64,512]{2,1,0:T(8,128)(2,1)S(1)} fusion(bf16[512,8,64]{0,2,1:T(8,128)(2,1)S(1)} %bitcast.197, f32[8,512,512]{1,2,0:T(8,128)} %fusion.159, f32[8,512,512]{1,2,0:T(8,128)} %copy-done.2, f32[8,512]{1,0:T(8,128)S(1)} %log_add_fusion, pred[512,512]{0,1:T(8,128)(4,1)S(1)} %broadcast_compare_fusion), kind=kOutput, calls=%fused_computation.113 | convolution fusion | flops 291770880 | bytes 18104320 | tf_op jit(solution)/shard_map/while/body/eval_jaxpr/hqk,khd->qhd/dot_general | solution.py:75
  471.4 13.6 %fusion.80 = bf16[8,64,512]{2,1,0:T(8,128)(2,1)S(1)} fusion(bf16[512,8,64]{0,2,1:T(8,128)(2,1)S(1)} %bitcast.195, f32[8,512,512]{1,2,0:T(8,128)} %fusion.159, f32[8,512,512]{1,2,0:T(8,128)} %copy-done.2, f32[8,512]{1,0:T(8,128)S(1)} %log_add_fusion, pred[512,512]{0,1:T(8,128)(4,1)S(1)} %broadcast_compare_fusion), kind=kOutput, calls=%fused_computation.114 | convolution fusion | flops 291770880 | bytes 18104320 | tf_op jit(solution)/shard_map/while/body/eval_jaxpr/hqk,qhd->khd/dot_general | solution.py:78
  485.1 5.9 convolution_convert_fusion.8
  491.0 2.9 convolution_convert_fusion
  494.2 4.5 fusion.161
  498.7 4.6 add_convert_fusion.1
  503.3 4.5 fusion.162
  507.9 4.7 add_convert_fusion
  512.9 3.5 fusion.99
  516.4 3.7 fusion.68
  520.1 4.8 copy.65
  527.7 40.6 %all-reduce = (f32[1024]{0:T(1024)}, f32[1024]{0:T(1024)}, f32[1024]{0:T(1024)}, f32[1024]{0:T(1024)}, f32[1024]{0:T(1024)}, /*index=5*/f32[1024]{0:T(1024)}) all-reduce(f32[1024]{0:T(1024)S(1)} %add.290, f32[1024]{0:T(1024)S(1)} %add.291, f32[1024]{0:T(1024)S(1)} %add.292, ...), channel_id=1, replica_groups=mesh['dp'=16,'tensor'=2] {'dp','tensor'}, use_global_device_ids=true, to_apply=%region_37.38 | all-reduce | flops 6144 | bytes 49152 | tf_op jit(solution)/shard_map/psum | solution.py:246
  571.7 60.7 %all-reduce.1 = (f32[1536]{0:T(1024)S(1)}, f32[2048]{0:T(1024)}) all-reduce(f32[1536]{0:T(1024)S(1)} %add.288, f32[2048]{0:T(1024)S(1)} %add.294), channel_id=1, replica_groups=mesh['dp'=16,'tensor'=2] {'dp'}, use_global_device_ids=true, to_apply=%region_33.34 | all-reduce | flops 3584 | bytes 28672 | tf_op jit(solution)/shard_map/psum | solution.py:245
  640.1 26.6 %reduce-scatter.35.cloned.1.call-done = bf16[2048,64]{0,1:T(8,128)(2,1)} async-done(((bf16[2048,1024]{0,1:T(8,128)(2,1)}), bf16[2048,64]{0,1:T(8,128)(2,1)}) %reduce-scatter.35.cloned.1.call-update) | async-done | bytes 262160 | tf_op jit(solution)/shard_map/reduce_scatter | solution.py:239
  668.5 67.8 %reduce-scatter.37.cloned.1.call-done = bf16[64,1536]{1,0:T(8,128)(2,1)} async-done(((bf16[1024,1536]{1,0:T(8,128)(2,1)}), bf16[64,1536]{1,0:T(8,128)(2,1)}) %reduce-scatter.37.cloned.1.call-update) | async-done | bytes 196624
  (255 shorter events, 79.8 us)
Async XLA Ops:
  7.2 62.7 %copy-start = (bf16[512,1024]{1,0:T(8,128)(2,1)S(1)}, bf16[512,1024]{1,0:T(8,128)(2,1)}, u32[]{:S(2)}) copy-start(bf16[512,1024]{1,0:T(8,128)(2,1)} %param.26) | copy-start | bytes 3145732
  7.2 5.6 copy-start.33
  7.2 5.7 copy-start.34
  7.2 27.0 %all-gather.25.cloned.1.call-start = ((), (), s32[]{:S(2)}) async-start(), calls=%async_computation.30 | async-start | bytes 1572864 | tf_op jit(solution)/shard_map/all_gather | solution.py:143
  9.7 48.0 %all-gather.23.cloned.1.call-start = ((), (), s32[]{:S(2)}) async-start(), calls=%async_computation.29 | async-start | bytes 1572864 | tf_op jit(solution)/shard_map/all_gather | solution.py:143
  10.4 81.6 %reduce-scatter.15.cloned.1.call-start = ((), (), s32[]{:S(2)}) async-start(), calls=%async_computation.12 | async-start | bytes 1572864 | tf_op jit(solution)/shard_map/reduce_scatter | solution.py:152
  11.4 53.8 %copy-start.13 = (pred[512,512]{0,1:T(8,128)(4,1)}, pred[512,512]{0,1:T(8,128)(4,1)S(1)}, u32[]{:S(2)}) copy-start(pred[512,512]{0,1:T(8,128)(4,1)S(1)} %broadcast_compare_fusion.1) | copy-start | bytes 786436
  38.5 33.4 %copy-start.18 = (bf16[512,512]{0,1:T(8,128)(2,1)}, bf16[512,512]{0,1:T(8,128)(2,1)S(1)}, u32[]{:S(2)}) copy-start(bf16[512,512]{0,1:T(8,128)(2,1)S(1)} %get-tuple-element.190) | copy-start | bytes 1572868
  38.5 33.4 %copy-start.20 = (bf16[512,512]{0,1:T(8,128)(2,1)}, bf16[512,512]{0,1:T(8,128)(2,1)S(1)}, u32[]{:S(2)}) copy-start(bf16[512,512]{0,1:T(8,128)(2,1)S(1)} %get-tuple-element.189) | copy-start | bytes 1572868
  38.5 36.7 %copy-start.22 = (bf16[512,512]{0,1:T(8,128)(2,1)}, bf16[512,512]{0,1:T(8,128)(2,1)S(1)}, u32[]{:S(2)}) copy-start(bf16[512,512]{0,1:T(8,128)(2,1)S(1)} %get-tuple-element.191) | copy-start | bytes 1572868
  71.6 43.6 %reduce-scatter.19.cloned.1.call-start = ((), (), s32[]{:S(2)}) async-start(), calls=%async_computation.15 | async-start | bytes 1572864 | tf_op jit(solution)/shard_map/reduce_scatter | solution.py:152
  76.6 5.0 copy-start.50
  79.0 13.1 %copy-start.1 = (bf16[2,256,1024]{2,1,0:T(8,128)(2,1)S(1)}, bf16[2,256,1024]{2,1,0:T(8,128)(2,1)}, u32[]{:S(2)}) copy-start(bf16[2,256,1024]{2,1,0:T(8,128)(2,1)} %param.18) | copy-start | bytes 3145732
  81.5 60.8 %all-gather.13.cloned.1.call-start = ((), (), s32[]{:S(2)}) async-start(), calls=%async_computation.16 | async-start | bytes 1572864 | tf_op jit(solution)/shard_map/all_gather | solution.py:158
  81.6 40.3 %copy-start.47 = (bf16[2048]{0:T(1024)(128)(2,1)S(1)}, bf16[2048]{0:T(1024)(128)(2,1)}, u32[]{:S(2)}) copy-start(bf16[2048]{0:T(1024)(128)(2,1)} %param.31) | copy-start | bytes 12292
  92.1 26.2 %copy-start.4 = (bf16[256,1024]{1,0:T(8,128)(2,1)S(1)}, bf16[256,1024]{1,0:T(8,128)(2,1)}, u32[]{:S(2)}) copy-start(bf16[256,1024]{1,0:T(8,128)(2,1)} %reduce-scatter.15.cloned.1.call-done) | copy-start | bytes 1572868
  120.9 44.8 %all-gather.11.cloned.1.call-start = ((), (), s32[]{:S(2)}) async-start(), calls=%async_computation.13 | async-start | bytes 1572864 | tf_op jit(solution)/shard_map/all_gather | solution.py:158
  121.5 93.3 %reduce-scatter.17.cloned.1.call-start = ((), (), s32[]{:S(2)}) async-start(), calls=%async_computation.14 | async-start | bytes 1572864 | tf_op jit(solution)/shard_map/reduce_scatter | solution.py:162
  165.7 25.3 %copy-start.56 = (bf16[2048,1024]{1,0:T(8,128)(2,1)S(1)}, bf16[2048,1024]{1,0:T(8,128)(2,1)}, u32[]{:S(2)}) copy-start(bf16[2048,1024]{1,0:T(8,128)(2,1)} %param.32) | copy-start | bytes 12582916
  194.3 43.7 %reduce-scatter.21.cloned.1.call-start = ((), (), s32[]{:S(2)}) async-start(), calls=%async_computation.17 | async-start | bytes 1572864 | tf_op jit(solution)/shard_map/reduce_scatter | solution.py:162
  194.4 6.5 copy-start.51
  194.4 6.5 copy-start.52
  194.4 6.5 copy-start.53
  194.4 43.6 %copy-start.5 = (bf16[256,1024]{1,0:T(8,128)(2,1)S(1)}, bf16[256,1024]{1,0:T(8,128)(2,1)}, u32[]{:S(2)}) copy-start(bf16[256,1024]{1,0:T(8,128)(2,1)} %reduce-scatter.19.cloned.1.call-done) | copy-start | bytes 1572868
  200.6 66.5 %all-gather.15.cloned.1.call-start = ((), (), s32[]{:S(2)}) async-start(), calls=%async_computation.18 | async-start | bytes 1572864 | tf_op jit(solution)/shard_map/all_gather | solution.py:172
  245.7 44.2 %all-gather.19.cloned.1.call-start = ((), (), s32[]{:S(2)}) async-start(), calls=%async_computation.22 | async-start | bytes 1572864 | tf_op jit(solution)/shard_map/all_gather | solution.py:172
  247.9 80.4 %reduce-scatter.27.cloned.1.call-start = ((), (), s32[]{:S(2)}) async-start(), calls=%async_computation.23 | async-start | bytes 1572864 | tf_op jit(solution)/shard_map/reduce_scatter | solution.py:178
  289.9 14.6 %copy-start.57 = (bf16[1024,2048]{1,0:T(8,128)(2,1)S(1)}, bf16[1024,2048]{1,0:T(8,128)(2,1)}, u32[]{:S(2)}) copy-start(bf16[1024,2048]{1,0:T(8,128)(2,1)} %param.30) | copy-start | bytes 12582916
  307.9 43.0 %reduce-scatter.23.cloned.1.call-start = ((), (), s32[]{:S(2)}) async-start(), calls=%async_computation.19 | async-start | bytes 1572864 | tf_op jit(solution)/shard_map/reduce_scatter | solution.py:178
  314.2 65.7 %all-gather.17.cloned.1.call-start = ((), (), s32[]{:S(2)}) async-start(), calls=%async_computation.20 | async-start | bytes 1572864 | tf_op jit(solution)/shard_map/all_gather | solution.py:188
  358.4 44.8 %all-gather.21.cloned.1.call-start = ((), (), s32[]{:S(2)}) async-start(), calls=%async_computation.24 | async-start | bytes 1572864 | tf_op jit(solution)/shard_map/all_gather | solution.py:188
  360.6 272.3 %reduce-scatter.31.cloned.1.call-start = ((), (), s32[]{:S(2)}) async-start(), calls=%async_computation.26 | async-start | bytes 1114112 | tf_op jit(solution)/shard_map/reduce_scatter | solution.py:236
  406.3 228.2 %reduce-scatter.25.cloned.1.call-start = ((), (), s32[]{:S(2)}) async-start(), calls=%async_computation.21 | async-start | bytes 1572864 | tf_op jit(solution)/shard_map/reduce_scatter | solution.py:205
  414.0 13.8 %copy-start.25 = (bf16[512,512]{0,1:T(8,128)(2,1)S(1)}, bf16[512,512]{0,1:T(8,128)(2,1)}, u32[]{:S(2)}) copy-start(bf16[512,512]{0,1:T(8,128)(2,1)} %copy-done.24) | copy-start | bytes 1572868
  427.8 85.1 %copy-start.38 = (bf16[8,64,512]{2,1,0:T(8,128)(2,1)}, bf16[8,64,512]{2,1,0:T(8,128)(2,1)S(1)}, u32[]{:S(2)}) copy-start(bf16[8,64,512]{2,1,0:T(8,128)(2,1)S(1)} %fusion.83) | copy-start | bytes 1572868
  427.8 14.5 %copy-start.42 = (bf16[512,512]{0,1:T(8,128)(2,1)S(1)}, bf16[512,512]{0,1:T(8,128)(2,1)}, u32[]{:S(2)}) copy-start(bf16[512,512]{0,1:T(8,128)(2,1)} %copy-done.41) | copy-start | bytes 1572868
  442.3 6.6 copy-start.39
  442.3 6.6 copy-start.45
  451.8 184.3 %reduce-scatter.29.cloned.1.call-start = ((), (), s32[]{:S(2)}) async-start(), calls=%async_computation.25 | async-start | bytes 1572864 | tf_op jit(solution)/shard_map/reduce_scatter | solution.py:205
  458.0 13.3 %copy-start.19 = (bf16[512,512]{0,1:T(8,128)(2,1)S(1)}, bf16[512,512]{0,1:T(8,128)(2,1)}, u32[]{:S(2)}) copy-start(bf16[512,512]{0,1:T(8,128)(2,1)} %copy-done.18) | copy-start | bytes 1572868
  471.4 45.0 %copy-start.15 = (bf16[8,64,512]{2,1,0:T(8,128)(2,1)}, bf16[8,64,512]{2,1,0:T(8,128)(2,1)S(1)}, u32[]{:S(2)}) copy-start(bf16[8,64,512]{2,1,0:T(8,128)(2,1)S(1)} %fusion.77) | copy-start | bytes 1572868
  485.1 31.4 %copy-start.16 = (bf16[8,64,512]{2,1,0:T(8,128)(2,1)}, bf16[8,64,512]{2,1,0:T(8,128)(2,1)S(1)}, u32[]{:S(2)}) copy-start(bf16[8,64,512]{2,1,0:T(8,128)(2,1)S(1)} %fusion.80) | copy-start | bytes 1572868
  485.1 5.9 copy-start.46
  491.0 25.4 %copy-start.17 = (bf16[8,64,512]{2,1,0:T(8,128)(2,1)}, bf16[8,64,512]{2,1,0:T(8,128)(2,1)S(1)}, u32[]{:S(2)}) copy-start(bf16[8,64,512]{2,1,0:T(8,128)(2,1)S(1)} %convolution_convert_fusion.8) | copy-start | bytes 1572868
  493.9 144.4 %reduce-scatter.33.cloned.1.call-start = ((), (), s32[]{:S(2)}) async-start(), calls=%async_computation.27 | async-start | bytes 4456448 | tf_op jit(solution)/shard_map/reduce_scatter | solution.py:233
  503.3 163.5 %reduce-scatter.35.cloned.1.call-start = ((), (), s32[]{:S(2)}) async-start(), calls=%async_computation.28 | async-start | bytes 4456448 | tf_op jit(solution)/shard_map/reduce_scatter | solution.py:239
  512.6 223.7 %reduce-scatter.37.cloned.1.call-start = ((), (), s32[]{:S(2)}) async-start(), calls=%async_computation.31 | async-start | bytes 3342336
  525.0 111.1 %copy-start.11 = (f32[256,1024]{1,0:T(8,128)S(1)}, f32[256,1024]{1,0:T(8,128)}, u32[]{:S(2)}) copy-start(f32[256,1024]{1,0:T(8,128)} %get-tuple-element.200) | copy-start | bytes 3145732
  (36 other events, 104.2 us)
Sparse Core Ops, SparseCore 0:
  10.2 23.9 all-gather.24
  36.3 21.2 all-gather.22
  71.7 20.3 reduce-scatter.14
  94.8 20.3 reduce-scatter.18
  121.0 21.2 all-gather.12
  144.3 21.2 all-gather.10
  194.5 20.3 reduce-scatter.16
  217.7 20.3 reduce-scatter.20
  245.8 21.2 all-gather.14
  268.6 21.2 all-gather.18
  308.0 20.3 reduce-scatter.26
  330.5 20.3 reduce-scatter.22
  358.5 21.2 all-gather.16
  381.8 21.2 all-gather.20
  406.6 57.3 reduce-scatter.30
  466.2 19.3 reduce-scatter.24
  494.0 20.5 reduce-scatter.28
  518.9 72.6 reduce-scatter.32
  595.4 71.3 reduce-scatter.34
  670.9 65.3 reduce-scatter.36
where the time goes:
time: 756 us; the launch traced here: 747 us
  waiting for transfers between devices  353 us (47%)
  matrix products  204 us (27%)
  blocking collectives  101 us (13%)
  other arithmetic  43.3 us (6%)
  local copies, waits for them, and re-layouts  27.1 us (4%)
  between operations  15.8 us (2%)
    unnamed x21, waiting for transfers between devices  69.3 us
    psum x1, blocking collectives, on_device(): bias_qkv, bias_up = lax.psum((small[0], small[1]), 'dp')  60.7 us
    dot_general x8, matrix products, matmul(): return jnp.dot(former, latter, preferred_element_type=jnp.float32)  51.9 us
    psum x1, blocking collectives, on_device(): lax.psum((small[2], small[3], small[4], small[5], small[6], small[7]), ('...  40.6 us
    all_gather x2, waiting for transfers between devices, on_device(): grad_one_rows = lax.all_gather(grad_one_low, 'tensor', axis=0, tiled=True)  40.3 us
    all_gather x2, waiting for transfers between devices, on_device(): full_rows = lax.all_gather(tokens_low, 'tensor', axis=0, tiled=True)  38.6 us
    dot_general x8, matrix products, inner_cols(): lax.dot_general(former, latter, (((1,), (1,)), ((), ())), preferred_eleme...  38.1 us
    reduce_scatter x2, waiting for transfers between devices, on_device(): lax.psum_scatter(matmul(gelu_low, w_down).astype(jnp.bfloat16), 'tensor',...  37.1 us
  transfers between devices with their start and end apart: 20, of which 16 were waited for; matrix products, arithmetic and copies ran while one was open for 24% of the time, Pallas kernels for 0%

commit v1 on v0

--- a/solution.py
+++ b/solution.py
@@ -7,6 +7,18 @@
 
 HD = 64
 MICRO = 2
+
+
+def collect(x, axis, dim):
+    ways, here = (lax.axis_size(axis), lax.axis_index(axis))
+    grown, reach = (x, 1)
+    while reach < ways:
+        theirs = lax.ppermute(grown, axis, [(d, d ^ reach) for d in range(ways)])
+        mine_first = jnp.concatenate([grown, theirs], axis=dim)
+        theirs_first = jnp.concatenate([theirs, grown], axis=dim)
+        grown = jnp.where(here & reach == 0, mine_first, theirs_first)
+        reach = 2 * reach
+    return grown
 
 
 def layer_norm(inputs, scale_vec, offset):
@@ -140,7 +152,7 @@
         tokens_low = hidden_in[micro_step]
         tokens = tokens_low.astype(jnp.float32)
         seg_rows = segment_ids[micro_step]
-        full_rows = lax.all_gather(tokens_low, "tensor", axis=0, tiled=True)
+        full_rows = collect(tokens_low, "tensor", 0)
         qkv_low = (matmul(full_rows, w_qkv) + b_qkv).astype(jnp.bfloat16)
         queries = qkv_low[:, :local_width]
         key_rows = qkv_low[:, local_width : 2 * local_width]

time: 756 us -> 742 us (0.981)
  waiting for transfers between devices: 353 us -> 326 us
    unnamed x21 -> x18, waiting for transfers between devices: 69.3 us -> 0.8 us
    reduce_scatter x0 -> x1, waiting for transfers between devices: none -> 67.7 us  [on_device(): lax.psum_scatter(summed[0].astype(jnp.bfloat16), 'dp', scatter_dimension=...]
    all_gather x2 -> x0, waiting for transfers between devices: 38.6 us -> none  [on_device(): full_rows = lax.all_gather(tokens_low, 'tensor', axis=0, tiled=True)]
    ppermute x0 -> x2, waiting for transfers between devices: none -> 10.6 us  [collect(): theirs = lax.ppermute(grown, axis, [(d, d ^ reach) for d in range(ways)])]
    unnamed x135 -> x132, local copies, waits for them, and re-layouts: 23.1 us -> 16.4 us
  transfers between devices with their start and end apart: 20 -> 20, of which waited for: 16 -> 16; matrix products, arithmetic and copies ran while one was open for 24% -> 25% of each run, Pallas kernels for 0% -> 0%
where the time goes in v1:
time: 742 us; the launch traced here: 733 us
  waiting for transfers between devices  326 us (44%)
  matrix products  208 us (28%)
  blocking collectives  102 us (14%)
  other arithmetic  43.1 us (6%)
  local copies, waits for them, and re-layouts  32.9 us (4%)
  between operations  15.7 us (2%)
    reduce_scatter x1, waiting for transfers between devices, on_device(): lax.psum_scatter(summed[0].astype(jnp.bfloat16), 'dp', scatter_dimension=...  67.7 us
    psum x1, blocking collectives, on_device(): bias_qkv, bias_up = lax.psum((small[0], small[1]), 'dp')  61.2 us
    dot_general x8, matrix products, matmul(): return jnp.dot(former, latter, preferred_element_type=jnp.float32)  52.3 us
    psum x1, blocking collectives, on_device(): lax.psum((small[2], small[3], small[4], small[5], small[6], small[7]), ('...  40.9 us
    all_gather x2, waiting for transfers between devices, on_device(): grad_one_rows = lax.all_gather(grad_one_low, 'tensor', axis=0, tiled=True)  40.3 us
    dot_general x8, matrix products, inner_cols(): lax.dot_general(former, latter, (((1,), (1,)), ((), ())), preferred_eleme...  38.1 us
    reduce_scatter x2, waiting for transfers between devices, on_device(): lax.psum_scatter(matmul(gelu_low, w_down).astype(jnp.bfloat16), 'tensor',...  37 us
    all_gather x2, waiting for transfers between devices, on_device(): hidden_rows = lax.all_gather(hidden_low, 'tensor', axis=0, tiled=True)  37 us
  transfers between devices with their start and end apart: 20, of which 16 were waited for; matrix products, arithmetic and copies ran while one was open for 25% of the time, Pallas kernels for 0%

profile of v1, /device:TPU:0, one launch (start us, length us, event | category | flops | bytes accessed | tf_op | source)
XLA Modules:
  0.0 733.4 jit_solution(10031405647437568592)
XLA Ops:
  9.7 2.9 collective-permute-start.1
  18.4 7.3 collective-permute-done.1
  25.7 4.3 fusion.69
  32.8 3.2 collective-permute-done
  36.1 4.3 fusion.68
  47.7 2.7 fusion.4
  68.6 11.9 %reduce-scatter.13.cloned.1.call-done = bf16[256,1024]{1,0:T(8,128)(2,1)} async-done(((bf16[512,1024]{1,0:T(8,128)(2,1)}), bf16[256,1024]{1,0:T(8,128)(2,1)}) %reduce-scatter.13.cloned.1.call-update) | async-done | bytes 524304 | tf_op jit(solution)/shard_map/reduce_scatter | solution.py:164
  81.9 21.9 %reduce-scatter.17.cloned.1.call-done = bf16[256,1024]{1,0:T(8,128)(2,1)} async-done(((bf16[512,1024]{1,0:T(8,128)(2,1)}), bf16[256,1024]{1,0:T(8,128)(2,1)}) %reduce-scatter.17.cloned.1.call-update) | async-done | bytes 524304 | tf_op jit(solution)/shard_map/reduce_scatter | solution.py:164
  110.5 20.4 %all-gather.9.cloned.1.call-done = bf16[512,1024]{1,0:T(8,128)(2,1)} async-done(((bf16[256,1024]{1,0:T(8,128)(2,1)}), bf16[512,1024]{1,0:T(8,128)(2,1)}) %all-gather.9.cloned.1.call-update) | async-done | bytes 1048592 | tf_op jit(solution)/shard_map/all_gather | solution.py:170
  130.9 6.8 fusion.152
  137.7 16.5 %all-gather.7.cloned.1.call-done = bf16[512,1024]{1,0:T(8,128)(2,1)} async-done(((bf16[256,1024]{1,0:T(8,128)(2,1)}), bf16[512,1024]{1,0:T(8,128)(2,1)}) %all-gather.7.cloned.1.call-update) | async-done | bytes 1048592 | tf_op jit(solution)/shard_map/all_gather | solution.py:170
  154.3 24.0 %multiply_convert_fusion.3 = (bf16[512,2048]{1,0:T(8,128)(2,1)S(1)}, f32[512,2048]{1,0:T(8,128)}, bf16[512,2048]{1,0:T(8,128)(2,1)}, f32[512,2048]{1,0:T(8,128)}, f32[512,2048]{1,0:T(8,128)}) fusion(f32[2048]{0:T(1024)S(1)} %convert_element_type.241, f32[512,2048]{1,0:T(8,128)} %fusion.152, bf16[512,1024]{1,0:T(8,128)(2,1)} %all-gather.7.cloned.1.call-done, ...), kind=kOutput, calls=%fused_computation.48 | convolution fusion | flops 2285895680 | bytes 26222592 | tf_op jit(solution)/shard_map/dot_general | solution.py:35
  179.6 3.3 convolution_convert_fusion.7
  183.0 6.2 convolution_convert_fusion.6
  189.5 13.9 %reduce-scatter.15.cloned.1.call-done = bf16[256,1024]{1,0:T(8,128)(2,1)} async-done(((bf16[512,1024]{1,0:T(8,128)(2,1)}), bf16[256,1024]{1,0:T(8,128)(2,1)}) %reduce-scatter.15.cloned.1.call-update) | async-done | bytes 524304 | tf_op jit(solution)/shard_map/reduce_scatter | solution.py:174
  203.4 23.1 %reduce-scatter.19.cloned.1.call-done = bf16[256,1024]{1,0:T(8,128)(2,1)} async-done(((bf16[512,1024]{1,0:T(8,128)(2,1)}), bf16[256,1024]{1,0:T(8,128)(2,1)}) %reduce-scatter.19.cloned.1.call-update) | async-done | bytes 524304 | tf_op jit(solution)/shard_map/reduce_scatter | solution.py:174
  236.4 19.2 %all-gather.11.cloned.1.call-done = bf16[512,1024]{1,0:T(8,128)(2,1)} async-done(((bf16[256,1024]{1,0:T(8,128)(2,1)}), bf16[512,1024]{1,0:T(8,128)(2,1)}) %all-gather.11.cloned.1.call-update) | async-done | bytes 1048592 | tf_op jit(solution)/shard_map/all_gather | solution.py:184
  255.6 6.9 fusion.153
  262.5 16.0 %all-gather.15.cloned.1.call-done = bf16[512,1024]{1,0:T(8,128)(2,1)} async-done(((bf16[256,1024]{1,0:T(8,128)(2,1)}), bf16[512,1024]{1,0:T(8,128)(2,1)}) %all-gather.15.cloned.1.call-update) | async-done | bytes 1048592 | tf_op jit(solution)/shard_map/all_gather | solution.py:184
  278.5 13.2 %convert_reduce_fusion = (f32[2048]{0:T(1024)S(1)}, bf16[512,2048]{1,0:T(8,128)(2,1)S(1)}, f32[2048]{0:T(1024)S(1)}, bf16[512,2048]{1,0:T(8,128)(2,1)}) fusion(f32[512,2048]{1,0:T(8,128)} %get-tuple-element.187, f32[512,2048]{1,0:T(8,128)} %fusion.152, f32[2048]{0:T(1024)S(1)} %convert_element_type.241, f32[512,2048]{1,0:T(8,128)} %fusion.153, ...), kind=kOutput, calls=%fused_computation.29 | convolution fusion | flops 2183131136 | bytes 30433280 | tf_op jit(solution)/shard_map/dot_general | solution.py:45
  293.1 3.4 convolution_convert_fusion.4
  296.5 6.2 convolution_convert_fusion.5
  302.8 14.1 %reduce-scatter.25.cloned.1.call-done = bf16[256,1024]{1,0:T(8,128)(2,1)} async-done(((bf16[512,1024]{1,0:T(8,128)(2,1)}), bf16[256,1024]{1,0:T(8,128)(2,1)}) %reduce-scatter.25.cloned.1.call-update) | async-done | bytes 524304 | tf_op jit(solution)/shard_map/reduce_scatter | solution.py:190
  316.9 22.5 %reduce-scatter.21.cloned.1.call-done = bf16[256,1024]{1,0:T(8,128)(2,1)} async-done(((bf16[512,1024]{1,0:T(8,128)(2,1)}), bf16[256,1024]{1,0:T(8,128)(2,1)}) %reduce-scatter.21.cloned.1.call-update) | async-done | bytes 524304 | tf_op jit(solution)/shard_map/reduce_scatter | solution.py:190
  339.5 3.3 multiply_reduce_fusion.3
  349.3 19.2 %all-gather.13.cloned.1.call-done = bf16[512,1024]{1,0:T(8,128)(2,1)} async-done(((bf16[256,1024]{1,0:T(8,128)(2,1)}), bf16[512,1024]{1,0:T(8,128)(2,1)}) %all-gather.13.cloned.1.call-update) | async-done | bytes 1048592 | tf_op jit(solution)/shard_map/all_gather | solution.py:200
  370.6 21.2 %all-gather.17.cloned.1.call-done = bf16[512,1024]{1,0:T(8,128)(2,1)} async-done(((bf16[256,1024]{1,0:T(8,128)(2,1)}), bf16[512,1024]{1,0:T(8,128)(2,1)}) %all-gather.17.cloned.1.call-update) | async-done | bytes 1048592 | tf_op jit(solution)/shard_map/all_gather | solution.py:200
  391.7 3.1 add_convert_fusion.5
  397.3 4.5 fusion.154
  401.8 14.6 %fusion.80 = bf16[8,64,512]{2,1,0:T(8,128)(2,1)} fusion(bf16[512,8,64]{0,2,1:T(8,128)(2,1)S(1)} %bitcast.179, f32[8,512,512]{1,2,0:T(8,128)} %fusion.154, f32[8,512,512]{1,2,0:T(8,128)} %copy-done.3, f32[8,512]{1,0:T(8,128)S(1)} %log_add_fusion.1, pred[512,512]{0,1:T(8,128)(4,1)S(1)} %copy-done.14), kind=kOutput, calls=%fused_computation.112 | convolution fusion | flops 291770880 | bytes 18104320 | tf_op jit(solution)/shard_map/while/body/eval_jaxpr/hqk,khd->qhd/dot_general | solution.py:87
  416.4 14.3 %fusion.83 = bf16[8,64,512]{2,1,0:T(8,128)(2,1)} fusion(bf16[512,8,64]{0,2,1:T(8,128)(2,1)S(1)} %bitcast.181, f32[8,512,512]{1,2,0:T(8,128)} %fusion.154, f32[8,512,512]{1,2,0:T(8,128)} %copy-done.3, f32[8,512]{1,0:T(8,128)S(1)} %log_add_fusion.1, pred[512,512]{0,1:T(8,128)(4,1)S(1)} %copy-done.14), kind=kOutput, calls=%fused_computation.113 | convolution fusion | flops 291770880 | bytes 18104320 | tf_op jit(solution)/shard_map/while/body/eval_jaxpr/hqk,qhd->khd/dot_general | solution.py:90
  430.7 5.7 convolution_convert_fusion.9
  437.3 2.8 convolution_convert_fusion.1
  442.0 4.5 fusion.155
  446.5 13.3 %fusion.74 = bf16[8,64,512]{2,1,0:T(8,128)(2,1)S(1)} fusion(bf16[512,8,64]{0,2,1:T(8,128)(2,1)S(1)} %bitcast.173, f32[8,512,512]{1,2,0:T(8,128)} %fusion.155, f32[8,512,512]{1,2,0:T(8,128)} %copy-done.2, f32[8,512]{1,0:T(8,128)S(1)} %log_add_fusion, pred[512,512]{0,1:T(8,128)(4,1)S(1)} %broadcast_compare_fusion), kind=kOutput, calls=%fused_computation.110 | convolution fusion | flops 291770880 | bytes 18104320 | tf_op jit(solution)/shard_map/while/body/eval_jaxpr/hqk,khd->qhd/dot_general | solution.py:87
  459.8 13.7 %fusion.77 = bf16[8,64,512]{2,1,0:T(8,128)(2,1)S(1)} fusion(bf16[512,8,64]{0,2,1:T(8,128)(2,1)S(1)} %bitcast.175, f32[8,512,512]{1,2,0:T(8,128)} %fusion.155, f32[8,512,512]{1,2,0:T(8,128)} %copy-done.2, f32[8,512]{1,0:T(8,128)S(1)} %log_add_fusion, pred[512,512]{0,1:T(8,128)(4,1)S(1)} %broadcast_compare_fusion), kind=kOutput, calls=%fused_computation.111 | convolution fusion | flops 291770880 | bytes 18104320 | tf_op jit(solution)/shard_map/while/body/eval_jaxpr/hqk,qhd->khd/dot_general | solution.py:90
  473.5 5.8 convolution_convert_fusion.8
  479.4 2.8 convolution_convert_fusion
  482.5 4.5 fusion.157
  487.0 4.6 add_convert_fusion.1
  492.8 4.2 fusion.158
  497.1 4.7 add_convert_fusion
  503.0 3.6 fusion.104
  506.6 5.3 add_convert_fusion.2
  514.6 40.9 %all-reduce = (f32[1024]{0:T(1024)}, f32[1024]{0:T(1024)}, f32[1024]{0:T(1024)}, f32[1024]{0:T(1024)}, f32[1024]{0:T(1024)}, /*index=5*/f32[1024]{0:T(1024)}) all-reduce(f32[1024]{0:T(1024)S(1)} %add.287, f32[1024]{0:T(1024)S(1)} %add.288, f32[1024]{0:T(1024)S(1)} %add.289, ...), channel_id=1, replica_groups=mesh['dp'=16,'tensor'=2] {'dp','tensor'}, use_global_device_ids=true, to_apply=%region_37.38 | all-reduce | flops 6144 | bytes 49152 | tf_op jit(solution)/shard_map/psum | solution.py:258
  558.9 61.2 %all-reduce.1 = (f32[1536]{0:T(1024)S(1)}, f32[2048]{0:T(1024)}) all-reduce(f32[1536]{0:T(1024)S(1)} %add.285, f32[2048]{0:T(1024)S(1)} %add.291), channel_id=1, replica_groups=mesh['dp'=16,'tensor'=2] {'dp'}, use_global_device_ids=true, to_apply=%region_33.34 | all-reduce | flops 3584 | bytes 28672 | tf_op jit(solution)/shard_map/psum | solution.py:257
  627.9 27.2 %reduce-scatter.35.cloned.1.call-done = bf16[2048,64]{0,1:T(8,128)(2,1)} async-done(((bf16[2048,1024]{0,1:T(8,128)(2,1)}), bf16[2048,64]{0,1:T(8,128)(2,1)}) %reduce-scatter.35.cloned.1.call-update) | async-done | bytes 262160 | tf_op jit(solution)/shard_map/reduce_scatter | solution.py:251
  656.8 67.7 %reduce-scatter.29.cloned.1.call-done = bf16[64,1536]{1,0:T(8,128)(2,1)} async-done(((bf16[1024,1536]{1,0:T(8,128)(2,1)}), bf16[64,1536]{1,0:T(8,128)(2,1)}) %reduce-scatter.29.cloned.1.call-update) | async-done | bytes 196624 | tf_op jit(solution)/shard_map/reduce_scatter | solution.py:242
  (256 shorter events, 90.7 us)
Async XLA Ops:
  7.2 49.6 %copy-start = (bf16[512,1024]{1,0:T(8,128)(2,1)S(1)}, bf16[512,1024]{1,0:T(8,128)(2,1)}, u32[]{:S(2)}) copy-start(bf16[512,1024]{1,0:T(8,128)(2,1)} %param.26) | copy-start | bytes 3145732
  7.2 8.5 %copy-start.27 = (bf16[1024,512]{1,0:T(8,128)(2,1)S(1)}, bf16[1024,512]{1,0:T(8,128)(2,1)}, u32[]{:S(2)}) copy-start(bf16[1024,512]{1,0:T(8,128)(2,1)} %param.23) | copy-start | bytes 3145732
  7.2 9.5 %copy-start.28 = (bf16[1024,512]{1,0:T(8,128)(2,1)S(1)}, bf16[1024,512]{1,0:T(8,128)(2,1)}, u32[]{:S(2)}) copy-start(bf16[1024,512]{1,0:T(8,128)(2,1)} %param.24) | copy-start | bytes 3145732
  7.2 10.7 %copy-start.54 = (bf16[512]{0:T(512)(128)(2,1)S(1)}, bf16[512]{0:T(512)(128)(2,1)}, u32[]{:S(2)}) copy-start(bf16[512]{0:T(512)(128)(2,1)} %param.25) | copy-start | bytes 3076
  7.2 10.6 %copy-start.55 = (bf16[512]{0:T(512)(128)(2,1)S(1)}, bf16[512]{0:T(512)(128)(2,1)}, u32[]{:S(2)}) copy-start(bf16[512]{0:T(512)(128)(2,1)} %param.22) | copy-start | bytes 3076
  7.2 73.3 %reduce-scatter.13.cloned.1.call-start = ((), (), s32[]{:S(2)}) async-start(), calls=%async_computation.12 | async-start | bytes 1572864 | tf_op jit(solution)/shard_map/reduce_scatter | solution.py:164
  9.7 16.0 %collective-permute-start.1 = (bf16[256,1024]{1,0:T(8,128)(2,1)}, bf16[256,1024]{1,0:T(8,128)(2,1)}, u32[]{:S(2)}, u32[]{:S(2)}) collective-permute-start(bf16[256,1024]{1,0:T(8,128)(2,1)} %get-tuple-element.177), channel_id=1, source_target_pairs={{0,1},{1,0},{2,3},{3,2},{4,5},{5,4},{6,7},{7,6},{8,9},{9,8},{10,11... | collective-permute-start | bytes 1572872 | tf_op jit(solution)/shard_map/ppermute | solution.py:16
  12.6 23.5 %collective-permute-start = (bf16[256,1024]{1,0:T(8,128)(2,1)}, bf16[256,1024]{1,0:T(8,128)(2,1)}, u32[]{:S(2)}, u32[]{:S(2)}) collective-permute-start(bf16[256,1024]{1,0:T(8,128)(2,1)} %get-tuple-element.178), channel_id=1, source_target_pairs={{0,1},{1,0},{2,3},{3,2},{4,5},{5,4},{6,7},{7,6},{8,9},{9,8},{10,11... | collective-permute-start | bytes 1572872 | tf_op jit(solution)/shard_map/ppermute | solution.py:16
  18.1 34.1 %copy-start.13 = (pred[512,512]{0,1:T(8,128)(4,1)}, pred[512,512]{0,1:T(8,128)(4,1)S(1)}, u32[]{:S(2)}) copy-start(pred[512,512]{0,1:T(8,128)(4,1)S(1)} %broadcast_compare_fusion.1) | copy-start | bytes 786436
  31.2 27.7 %copy-start.15 = (bf16[512,512]{0,1:T(8,128)(2,1)}, bf16[512,512]{0,1:T(8,128)(2,1)S(1)}, u32[]{:S(2)}) copy-start(bf16[512,512]{0,1:T(8,128)(2,1)S(1)} %copy.61) | copy-start | bytes 1572868
  31.4 27.4 %copy-start.17 = (bf16[512,512]{0,1:T(8,128)(2,1)}, bf16[512,512]{0,1:T(8,128)(2,1)S(1)}, u32[]{:S(2)}) copy-start(bf16[512,512]{0,1:T(8,128)(2,1)S(1)} %copy.60) | copy-start | bytes 1572868
  32.8 29.2 %copy-start.19 = (bf16[512,512]{0,1:T(8,128)(2,1)}, bf16[512,512]{0,1:T(8,128)(2,1)S(1)}, u32[]{:S(2)}) copy-start(bf16[512,512]{0,1:T(8,128)(2,1)S(1)} %copy.59) | copy-start | bytes 1572868
  58.5 45.2 %reduce-scatter.17.cloned.1.call-start = ((), (), s32[]{:S(2)}) async-start(), calls=%async_computation.15 | async-start | bytes 1572864 | tf_op jit(solution)/shard_map/reduce_scatter | solution.py:164
  65.9 14.6 %copy-start.1 = (bf16[2,256,1024]{2,1,0:T(8,128)(2,1)S(1)}, bf16[2,256,1024]{2,1,0:T(8,128)(2,1)}, u32[]{:S(2)}) copy-start(bf16[2,256,1024]{2,1,0:T(8,128)(2,1)} %param.18) | copy-start | bytes 3145732
  68.5 62.5 %all-gather.9.cloned.1.call-start = ((), (), s32[]{:S(2)}) async-start(), calls=%async_computation.16 | async-start | bytes 1572864 | tf_op jit(solution)/shard_map/all_gather | solution.py:170
  68.6 41.9 %copy-start.47 = (bf16[2048]{0:T(1024)(128)(2,1)S(1)}, bf16[2048]{0:T(1024)(128)(2,1)}, u32[]{:S(2)}) copy-start(bf16[2048]{0:T(1024)(128)(2,1)} %param.31) | copy-start | bytes 12292
  80.5 26.3 %copy-start.4 = (bf16[256,1024]{1,0:T(8,128)(2,1)S(1)}, bf16[256,1024]{1,0:T(8,128)(2,1)}, u32[]{:S(2)}) copy-start(bf16[256,1024]{1,0:T(8,128)(2,1)} %reduce-scatter.13.cloned.1.call-done) | copy-start | bytes 1572868
  109.5 44.8 %all-gather.7.cloned.1.call-start = ((), (), s32[]{:S(2)}) async-start(), calls=%async_computation.13 | async-start | bytes 1572864 | tf_op jit(solution)/shard_map/all_gather | solution.py:170
  110.0 93.4 %reduce-scatter.15.cloned.1.call-start = ((), (), s32[]{:S(2)}) async-start(), calls=%async_computation.14 | async-start | bytes 1572864 | tf_op jit(solution)/shard_map/reduce_scatter | solution.py:174
  154.3 25.3 %copy-start.56 = (bf16[2048,1024]{1,0:T(8,128)(2,1)S(1)}, bf16[2048,1024]{1,0:T(8,128)(2,1)}, u32[]{:S(2)}) copy-start(bf16[2048,1024]{1,0:T(8,128)(2,1)} %param.32) | copy-start | bytes 12582916
  182.9 43.6 %reduce-scatter.19.cloned.1.call-start = ((), (), s32[]{:S(2)}) async-start(), calls=%async_computation.17 | async-start | bytes 1572864 | tf_op jit(solution)/shard_map/reduce_scatter | solution.py:174
  183.0 6.5 copy-start.51
  183.0 6.5 copy-start.52
  183.0 6.5 copy-start.53
  183.0 43.5 %copy-start.5 = (bf16[256,1024]{1,0:T(8,128)(2,1)S(1)}, bf16[256,1024]{1,0:T(8,128)(2,1)}, u32[]{:S(2)}) copy-start(bf16[256,1024]{1,0:T(8,128)(2,1)} %reduce-scatter.17.cloned.1.call-done) | copy-start | bytes 1572868
  189.2 66.4 %all-gather.11.cloned.1.call-start = ((), (), s32[]{:S(2)}) async-start(), calls=%async_computation.18 | async-start | bytes 1572864 | tf_op jit(solution)/shard_map/all_gather | solution.py:184
  234.2 44.3 %all-gather.15.cloned.1.call-start = ((), (), s32[]{:S(2)}) async-start(), calls=%async_computation.22 | async-start | bytes 1572864 | tf_op jit(solution)/shard_map/all_gather | solution.py:184
  236.4 80.6 %reduce-scatter.25.cloned.1.call-start = ((), (), s32[]{:S(2)}) async-start(), calls=%async_computation.23 | async-start | bytes 1572864 | tf_op jit(solution)/shard_map/reduce_scatter | solution.py:190
  278.5 14.6 %copy-start.57 = (bf16[1024,2048]{1,0:T(8,128)(2,1)S(1)}, bf16[1024,2048]{1,0:T(8,128)(2,1)}, u32[]{:S(2)}) copy-start(bf16[1024,2048]{1,0:T(8,128)(2,1)} %param.30) | copy-start | bytes 12582916
  296.5 43.0 %reduce-scatter.21.cloned.1.call-start = ((), (), s32[]{:S(2)}) async-start(), calls=%async_computation.19 | async-start | bytes 1572864 | tf_op jit(solution)/shard_map/reduce_scatter | solution.py:190
  302.8 65.7 %all-gather.13.cloned.1.call-start = ((), (), s32[]{:S(2)}) async-start(), calls=%async_computation.20 | async-start | bytes 1572864 | tf_op jit(solution)/shard_map/all_gather | solution.py:200
  346.9 44.8 %all-gather.17.cloned.1.call-start = ((), (), s32[]{:S(2)}) async-start(), calls=%async_computation.24 | async-start | bytes 1572864 | tf_op jit(solution)/shard_map/all_gather | solution.py:200
  349.2 271.5 %reduce-scatter.31.cloned.1.call-start = ((), (), s32[]{:S(2)}) async-start(), calls=%async_computation.27 | async-start | bytes 1114112 | tf_op jit(solution)/shard_map/reduce_scatter | solution.py:248
  394.9 227.3 %reduce-scatter.23.cloned.1.call-start = ((), (), s32[]{:S(2)}) async-start(), calls=%async_computation.21 | async-start | bytes 1572864 | tf_op jit(solution)/shard_map/reduce_scatter | solution.py:217
  401.8 14.6 %copy-start.22 = (bf16[512,512]{0,1:T(8,128)(2,1)S(1)}, bf16[512,512]{0,1:T(8,128)(2,1)}, u32[]{:S(2)}) copy-start(bf16[512,512]{0,1:T(8,128)(2,1)} %copy.56) | copy-start | bytes 1572868
  430.7 6.6 copy-start.32
  430.7 6.6 copy-start.34
  430.7 6.6 copy-start.45
  440.2 183.6 %reduce-scatter.27.cloned.1.call-start = ((), (), s32[]{:S(2)}) async-start(), calls=%async_computation.25 | async-start | bytes 1572864 | tf_op jit(solution)/shard_map/reduce_scatter | solution.py:217
  446.5 13.3 %copy-start.18 = (bf16[512,512]{0,1:T(8,128)(2,1)S(1)}, bf16[512,512]{0,1:T(8,128)(2,1)}, u32[]{:S(2)}) copy-start(bf16[512,512]{0,1:T(8,128)(2,1)} %copy-done.17) | copy-start | bytes 1572868
  459.8 19.5 %copy-start.38 = (bf16[8,64,512]{2,1,0:T(8,128)(2,1)}, bf16[8,64,512]{2,1,0:T(8,128)(2,1)S(1)}, u32[]{:S(2)}) copy-start(bf16[8,64,512]{2,1,0:T(8,128)(2,1)S(1)} %fusion.74) | copy-start | bytes 1572868
  459.8 13.7 %copy-start.44 = (bf16[512,512]{0,1:T(8,128)(2,1)S(1)}, bf16[512,512]{0,1:T(8,128)(2,1)}, u32[]{:S(2)}) copy-start(bf16[512,512]{0,1:T(8,128)(2,1)} %copy-done.43) | copy-start | bytes 1572868
  473.5 5.8 copy-start.40
  473.5 5.8 copy-start.46
  482.3 143.8 %reduce-scatter.33.cloned.1.call-start = ((), (), s32[]{:S(2)}) async-start(), calls=%async_computation.28 | async-start | bytes 4456448 | tf_op jit(solution)/shard_map/reduce_scatter | solution.py:245
  491.6 163.4 %reduce-scatter.35.cloned.1.call-start = ((), (), s32[]{:S(2)}) async-start(), calls=%async_computation.29 | async-start | bytes 4456448 | tf_op jit(solution)/shard_map/reduce_scatter | solution.py:251
  501.8 222.7 %reduce-scatter.29.cloned.1.call-start = ((), (), s32[]{:S(2)}) async-start(), calls=%async_computation.26 | async-start | bytes 3342336 | tf_op jit(solution)/shard_map/reduce_scatter | solution.py:242
  512.0 111.8 %copy-start.11 = (f32[256,1024]{1,0:T(8,128)S(1)}, f32[256,1024]{1,0:T(8,128)}, u32[]{:S(2)}) copy-start(f32[256,1024]{1,0:T(8,128)} %get-tuple-element.166) | copy-start | bytes 3145732
  (37 other events, 113.5 us)
Sparse Core Ops, SparseCore 0:
  58.7 21.7 reduce-scatter.12
  83.4 20.3 reduce-scatter.16
  109.6 21.3 all-gather.8
  132.9 21.2 all-gather.6
  183.0 20.3 reduce-scatter.14
  206.2 20.3 reduce-scatter.18
  234.3 21.2 all-gather.10
  257.2 21.2 all-gather.14
  296.6 20.3 reduce-scatter.24
  319.1 20.3 reduce-scatter.20
  347.1 21.2 all-gather.12
  370.4 21.2 all-gather.16
  395.3 57.3 reduce-scatter.30
  455.0 19.3 reduce-scatter.22
  482.4 20.5 reduce-scatter.26
  507.2 72.8 reduce-scatter.32
  583.8 71.2 reduce-scatter.34
  659.2 65.2 reduce-scatter.28
